TPU v7x, 256 devices: a whole 4x4x8 slice. The times are simulated.
256 devices in a mesh: rows: 32 (over z, y), span: 8 (over x, core).
Axes of the slice: x: 4, y: 4, z: 8, core: 2. Of those that a mesh axis runs over, the one named last changes fastest.
Arguments:
- rotor_face: bfloat16 [8, 256, 160, 128], P('span', 'rows'), may hold values from -6 to 6
- pair_source: int32 [8, 1024, 1], P('span', 'rows'), may hold values from 0 to 31; in each aligned block of 32 rows (0 to 31, 32 to 63, ..., all dimensions but the last counted through in order) at most 2 rows name the same one
- pair_block: int32 [8, 1024], P('span', 'rows'), may hold values from 0 to 7
- pair_row: int32 [8, 1024], P('span', 'rows'), may hold values from 0 to 7
- pair_weight: bfloat16 [8, 1024, 128, 128], P('span', 'rows'), may hold values from -0.5 to 0.5
- stator_field: float32 [4, 160, 64, 4096], P(None, None, 'span', 'rows'), may hold values from -6 to 6
- damping: float32 [64, 4096], P('span', 'rows'), may hold values from 0.05 to 0.5
Outputs:
- interface: float32 [160, 64, 4096], P(None, 'span', 'rows')
- updated: float32 [4, 160, 64, 4096], P(None, None, 'span', 'rows')
Inputs may be any that keep to these rules, and one draw needn't show every extreme that they name: `pair_source`: among the pairs of one receiving device, no source index appears more than 2 times; in every draw some device names one source exactly 2 times.
All inputs are finite; a program needn't handle non-finite values.
Results may differ from a plain program's by a relative error of at most 0.0003.
Values may be sent and summed in bfloat16 or wider, within the bound.
No kernel may reach another device: no remote copies, remote signals or barrier semaphores. Data moves between devices by JAX's collectives and lax.ppermute only.
A program may use at most 128 MiB of HBM per device.

v0:
```python
import jax
import jax.numpy as jnp
from jax import lax
from jax.sharding import PartitionSpec as P

NVAR = 5
STEPS = 2


UPWIND = 0.45
DIFFUSE = 0.2
TURNING = 0.02


def padded_2(cells, sides, width, closed):
    for axis, dim in sides:
        count = lax.axis_size(axis)
        ends = count if closed else count - 1
        head = lax.slice_in_dim(cells, 0, width, axis=dim)
        tail = lax.slice_in_dim(cells, cells.shape[dim] - width, cells.shape[dim], axis=dim)
        cells = jnp.concatenate(
            [
                lax.ppermute(tail, axis, [(i, (i + 1) % count) for i in range(ends)]),
                cells,
                lax.ppermute(head, axis, [((i + 1) % count, i) for i in range(ends)]),
            ],
            axis=dim,
        )
    return cells


def harmonic_turn(field, nvars):
    shape = field.shape
    split = field.reshape(shape[0], nvars, -1, 2, shape[2], shape[3])
    count = split.shape[2]
    order = (jnp.arange(count, dtype=jnp.float32) + 1.0).reshape(1, 1, count, 1, 1)
    real_part = split[:, :, :, 0]
    imag_part = split[:, :, :, 1]
    return jnp.stack([order * imag_part, -order * real_part], axis=3).reshape(shape)


def advance(padded, face_ext, damp_ext, first_row, span_total):
    inner = padded[:, :, 1:-1, 1:-1]
    beside = (
        padded[:, :, 2:, 1:-1]
        + padded[:, :, :-2, 1:-1]
        + padded[:, :, 1:-1, 2:]
        + padded[:, :, 1:-1, :-2]
    )
    upstream = jnp.concatenate([face_ext[None, :, 1:-1, 1:-1], inner[:-1]], axis=0)
    damp = damp_ext[1:-1, 1:-1]
    updated = (
        inner
        + UPWIND * (upstream - inner)
        + DIFFUSE * (beside - 4.0 * inner)
        - damp * inner
        + TURNING * harmonic_turn(inner, NVAR)
    )
    global_rows = first_row + 1 + jnp.arange(inner.shape[2], dtype=jnp.int32)
    inside = ((global_rows >= 0) & (global_rows < span_total)).astype(jnp.float32)
    return updated * inside[None, None, :, None]


def per_device(rotor_face, pair_source, pair_block, pair_row, pair_weight, stator_field, damping):
    coefs = rotor_face.shape[2]
    width = rotor_face.shape[3]
    pairs_dev = pair_block.shape[1]
    layers = stator_field.shape[0]
    span_rows = stator_field.shape[2]
    devices_rows = lax.axis_size("rows")
    capacity = max(2, 2 * pairs_dev // devices_rows)
    sources = pair_source[0, :, 0]
    local_blocks = pair_block[0]
    targets = pair_row[0]
    weights = pair_weight[0]
    own_faces = rotor_face[0]
    pair_ids = jnp.arange(pairs_dev, dtype=jnp.int32)
    earlier = (sources[None, :] == sources[:, None]) & (pair_ids[None, :] < pair_ids[:, None])
    ranks = jnp.sum(earlier.astype(jnp.int32), axis=1)
    slots = sources * capacity + ranks
    slot_ids = jnp.arange(devices_rows * capacity, dtype=jnp.int32)
    slot_hits = (slots[None, :] == slot_ids[:, None]).astype(jnp.int32)
    wanted = jnp.sum(slot_hits * local_blocks[None, :], axis=1).reshape(devices_rows, capacity)
    asked = lax.all_to_all(wanted, "rows", split_axis=0, concat_axis=0, tiled=True)
    reply = jnp.take(own_faces, asked.reshape(-1), axis=0)
    arrived = lax.all_to_all(reply, "rows", split_axis=0, concat_axis=0, tiled=True)
    chosen = jnp.take(arrived, slots, axis=0)
    terms = jnp.einsum("pck,pki->pci", chosen, weights, preferred_element_type=jnp.float32)
    row_hits = (targets[:, None] == jnp.arange(span_rows, dtype=jnp.int32)[None, :]).astype(
        jnp.float32
    )
    interface = jnp.einsum("pr,pci->cri", row_hits, terms, precision=lax.Precision.HIGHEST)
    span_total = span_rows * lax.axis_size("span")
    span_first = lax.axis_index("span") * span_rows
    field = stator_field
    face_ext = jnp.pad(interface, ((0, 0), (1, 1), (1, 1)))
    damp_ext = jnp.pad(damping, 1)
    for section in range(STEPS):
        flat = field.reshape(layers * coefs, span_rows, width)
        grown = padded_2(flat, (("span", 1),), 1, False)
        grown = padded_2(grown, (("rows", 2),), 1, True)
        padded = grown.reshape(layers, coefs, span_rows + 2, width + 2)
        field = advance(padded, face_ext, damp_ext, span_first - 1, span_total)
    return (interface, field)


def solution(mesh):
    placed = (
        P("span", "rows", None, None),
        P("span", "rows", None),
        P("span", "rows"),
        P("span", "rows"),
        P("span", "rows", None, None),
        P(None, None, "span", "rows"),
        P("span", "rows"),
    )
    return jax.shard_map(
        per_device,
        mesh=mesh,
        in_specs=placed,
        out_specs=(P(None, "span", "rows"), P(None, None, "span", "rows")),
        check_vma=False,
    )
```

profile of v0, /device:TPU:1, one launch (start us, length us, event | category | flops | bytes accessed | tf_op | source)
XLA Modules:
  0.0 211.0 jit_solution(12401654501047214074)
XLA Ops:
  0.6 0.9 convert_reduce_fusion
  1.6 0.7 compare_and_fusion.1
  2.3 0.7 select_reduce_fusion
  3.1 20.4 %all_to_all.14 = s32[32,1,2]{2,1,0:T(1,128)S(1)} all-to-all(s32[32,1,2]{2,1,0:T(1,128)S(1)} %bitcast.56), channel_id=1, replica_groups=mesh['rows'=32,'span'=8] {'rows'}, dimensions={0} | all-to-all | bytes 512 | tf_op jit(solution)/shard_map/all_to_all | solution.py:84
  23.7 0.5 broadcast.149
  24.2 0.7 reduce.5
  25.0 3.3 %gather_fusion = bf16[64,160,128]{2,1,0:T(8,128)(2,1)} fusion(bf16[8,160,128]{2,1,0:T(8,128)(2,1)} %bitcast.44, s32[1024]{0:T(1024)S(1)} %pad_clamp_fusion.1), kind=kCustom, calls=%fused_computation | custom fusion | bytes 5243136 | tf_op jit(solution)/shard_map/jit(_take)/gather | solution.py:85
  28.3 3.5 %broadcast_select_fusion = bf16[64,160,128]{2,1,0:T(8,128)(2,1)} fusion(bf16[64,160,128]{2,1,0:T(8,128)(2,1)} %gather_fusion, pred[64]{0:T(512)(128)(4,1)S(1)} %compare_and_fusion), kind=kLoop, calls=%fused_computation.36 | loop fusion | flops 1310720 | bytes 5242944 | tf_op jit(solution)/shard_map/jit(_take)/select_n | solution.py:85
  31.9 4.9 %all-to-all-start.1 = ((bf16[64,160,128]{2,1,0:T(8,128)(2,1)}), bf16[64,160,128]{2,1,0:T(8,128)(2,1)}, u32[]{:S(2)}, u32[]{:S(2)}) async-start(bf16[64,160,128]{2,1,0:T(8,128)(2,1)} %broadcast_select_fusion), calls=%async_computation.1 | async-start | bytes 5242880 | tf_op jit(solution)/shard_map/all_to_all | solution.py:86
  36.8 3.0 %fusion.36 = (f32[640,1,128]{2,1,0:T(1,128)S(1)}, f32[640,1,128]{2,1,0:T(1,128)S(1)}) fusion(f32[640,8,128]{2,1,0:T(8,128)} %bitcast.45), kind=kLoop, calls=%fused_computation.73 | loop fusion | bytes 1310720 | tf_op jit(solution)/shard_map/slice | solution.py:20
  39.8 5.1 %collective-permute-start = (f32[640,1,128]{2,1,0:T(1,128)S(1)}, f32[640,1,128]{2,1,0:T(1,128)S(1)}, u32[]{:S(2)}, u32[]{:S(2)}) collective-permute-start(f32[640,1,128]{2,1,0:T(1,128)S(1)} %get-tuple-element.14), channel_id=1, source_target_pairs={{0,1},{1,2},{2,3},{3,4},{4,5},{5,6},{6,7},{8,9},{9,10},{10,11},{11... | collective-permute-start | bytes 983048 | tf_op jit(solution)/shard_map/ppermute | solution.py:23
  45.0 1.9 collective-permute-start.1
  46.9 2.0 collective-permute-done
  49.0 4.8 %collective-permute-done.1 = f32[640,1,128]{2,1,0:T(1,128)S(1)} collective-permute-done((f32[640,1,128]{2,1,0:T(1,128)S(1)}, f32[640,1,128]{2,1,0:T(1,128)S(1)}, u32[]{:S(2)}, u32[]{:S(2)}) %collective-permute-start.1) | collective-permute-done | bytes 327712 | tf_op jit(solution)/shard_map/ppermute | solution.py:25
  53.7 2.6 %pad_maximum_fusion.2 = f32[640,10,128]{2,1,0:T(8,128)S(1)} fusion(f32[640,1,128]{2,1,0:T(1,128)S(1)} %collective-permute-done.1, f32[640,8,128]{2,1,0:T(8,128)} %bitcast.46, f32[640,1,128]{2,1,0:T(1,128)S(1)} %collective-permute-done), kind=kLoop, calls=%fused_computation.4 | loop fusion | flops 1638400 | bytes 6553600 | tf_op jit(solution)/shard_map/concatenate | solution.py:21
  56.4 5.7 %fusion.34 = (f32[640,10,1]{2,1,0:T(8,128)}, f32[640,10,1]{2,1,0:T(8,128)}) fusion(f32[640,10,128]{2,1,0:T(8,128)S(1)} %pad_maximum_fusion.2), kind=kLoop, calls=%fused_computation.71 | loop fusion | bytes 102400 | tf_op jit(solution)/shard_map/slice | solution.py:20
  62.1 3.3 %copy.37 = f32[640,10,1]{0,2,1:T(1,128)S(1)} copy(f32[640,10,1]{2,1,0:T(8,128)} %get-tuple-element.6) | data formatting | bytes 51200 | tf_op jit(solution)/shard_map/slice | solution.py:20
  65.4 3.3 %copy.38 = f32[640,10,1]{0,2,1:T(1,128)S(1)} copy(f32[640,10,1]{2,1,0:T(8,128)} %get-tuple-element.7) | data formatting | bytes 51200 | tf_op jit(solution)/shard_map/slice | solution.py:19
  68.7 4.9 %collective-permute-start.3 = (f32[640,10,1]{0,2,1:T(1,128)S(1)}, f32[640,10,1]{0,2,1:T(1,128)S(1)}, u32[]{:S(2)}, u32[]{:S(2)}) collective-permute-start(f32[640,10,1]{0,2,1:T(1,128)S(1)} %copy.38), channel_id=1, source_target_pairs={{8,0},{16,8},{24,16},{32,24},{40,32},{48,40},{56,48},{64,56},{72,6... | collective-permute-start | bytes 76808 | tf_op jit(solution)/shard_map/ppermute | solution.py:25
  73.6 21.6 %collective-permute-done.2 = f32[640,10,1]{0,2,1:T(1,128)S(1)} collective-permute-done((f32[640,10,1]{0,2,1:T(1,128)S(1)}, f32[640,10,1]{0,2,1:T(1,128)S(1)}, u32[]{:S(2)}, u32[]{:S(2)}) %collective-permute-start.2) | collective-permute-done | bytes 25632 | tf_op jit(solution)/shard_map/ppermute | solution.py:23
  95.3 3.2 %copy.39 = f32[640,10,1]{2,1,0:T(8,128)} copy(f32[640,10,1]{0,2,1:T(1,128)S(1)} %collective-permute-done.2) | data formatting | bytes 51200 | tf_op jit(solution)/shard_map/ppermute | solution.py:23
  98.5 3.2 %copy.40 = f32[640,10,1]{2,1,0:T(8,128)} copy(f32[640,10,1]{0,2,1:T(1,128)S(1)} %collective-permute-done.3) | data formatting | bytes 51200 | tf_op jit(solution)/shard_map/ppermute | solution.py:25
  101.6 10.8 %pad_maximum_fusion = f32[640,10,130]{2,1,0:T(8,128)S(1)} fusion(f32[640,10,1]{2,1,0:T(8,128)} %copy.40, f32[640,1,128]{2,1,0:T(1,128)S(1)} %collective-permute-done.1, f32[640,8,128]{2,1,0:T(8,128)} %bitcast.47, f32[640,1,128]{2,1,0:T(1,128)S(1)} %collective-permute-done, f32[640,10,1]{2,1,0:T(8,128)} %copy.39), kind=kLoop, calls=%fused_computation.2 | loop fusion | flops 3328000 | bytes 6656000 | tf_op jit(solution)/shard_map/concatenate | solution.py:21
  112.4 2.2 %slice.111 = f32[3,160,8,128]{3,2,1,0:T(8,128)} slice(f32[4,160,10,130]{3,2,1,0:T(8,128)S(1)} %bitcast.35), slice={[0:3], [0:160], [1:9], [1:129]} | slice | bytes 3932160 | tf_op jit(solution)/shard_map/slice | solution.py:50
  114.6 2.3 %copy-done.2 = f32[640,10,130]{2,1,0:T(8,128)} copy-done((f32[640,10,130]{2,1,0:T(8,128)}, f32[640,10,130]{2,1,0:T(8,128)S(1)}, u32[]{:S(2)}) %copy-start.2) | copy-done | bytes 3328024
  116.9 0.7 slice.110
  117.7 0.4 slice_multiply_fusion.3
  118.1 1.8 maximum_multiply_fusion
  119.9 2.5 %gather_fusion.1 = bf16[32,160,128]{2,1,0:T(8,128)(2,1)S(1)} fusion(bf16[64,160,128]{2,1,0:T(8,128)(2,1)} %all-to-all-done.1, s32[1024]{0:T(1024)S(1)} %pad_clamp_fusion), kind=kCustom, calls=%fused_computation.1 | custom fusion | bytes 2621568 | tf_op jit(solution)/shard_map/jit(_take)/gather | solution.py:87
  122.5 0.6 fusion.20
  123.1 2.4 %fusion.18 = f32[160,128,8]{1,2,0:T(8,128)S(1)} fusion(f32[32,160,128]{2,1,0:T(8,128)S(1)} %fusion.20, s32[32]{0:T(128)S(1)} %bitcast.58), kind=kOutput, calls=%fused_computation.34 | convolution fusion | flops 62914816 | bytes 3276928 | tf_op jit(solution)/shard_map/pr,pci->cri/dot_general | solution.py:92
  125.6 15.9 %fusion.6 = f32[4,160,8,128]{3,2,1,0:T(8,128)S(1)} fusion(f32[4,160,8,128]{3,2,1,0:T(8,128)S(1)} %bitcast.48, f32[1,160,8,128]{3,2,1,0:T(8,128)S(1)} %bitcast.52, f32[4,160,10,130]{3,2,1,0:T(8,128)} %bitcast.37, f32[3,160,8,128]{3,2,1,0:T(8,128)} %slice.111, f32[8]{0:T(128)S(1)} %and_convert_fusion, f32[8,128]{1,0:T(8,128)S(1)} %copy-done.8), kind=kLoop, calls=%fused_computation.14 | loop fusion | flops 9830400 | bytes 20975648 | tf_op jit(solution)/shard_map/mul | solution.py:61
  141.9 5.0 %collective-permute-start.4 = (f32[640,1,128]{2,1,0:T(1,128)S(1)}, f32[640,1,128]{2,1,0:T(1,128)S(1)}, u32[]{:S(2)}, u32[]{:S(2)}) collective-permute-start(f32[640,1,128]{2,1,0:T(1,128)S(1)} %get-tuple-element.10), channel_id=1, source_target_pairs={{0,1},{1,2},{2,3},{3,4},{4,5},{5,6},{6,7},{8,9},{9,10},{10,11},{11... | collective-permute-start | bytes 983048 | tf_op jit(solution)/shard_map/ppermute | solution.py:23
  146.8 2.1 %collective-permute-start.5 = (f32[640,1,128]{2,1,0:T(1,128)S(1)}, f32[640,1,128]{2,1,0:T(1,128)S(1)}, u32[]{:S(2)}, u32[]{:S(2)}) collective-permute-start(f32[640,1,128]{2,1,0:T(1,128)S(1)} %get-tuple-element.11), channel_id=1, source_target_pairs={{1,0},{2,1},{3,2},{4,3},{5,4},{6,5},{7,6},{9,8},{10,9},{11,10},{12... | collective-permute-start | bytes 983048 | tf_op jit(solution)/shard_map/ppermute | solution.py:25
  149.0 1.8 collective-permute-done.4
  150.8 4.4 %collective-permute-done.5 = f32[640,1,128]{2,1,0:T(1,128)S(1)} collective-permute-done((f32[640,1,128]{2,1,0:T(1,128)S(1)}, f32[640,1,128]{2,1,0:T(1,128)S(1)}, u32[]{:S(2)}, u32[]{:S(2)}) %collective-permute-start.5) | collective-permute-done | bytes 327712 | tf_op jit(solution)/shard_map/ppermute | solution.py:25
  155.2 1.0 pad_maximum_fusion.3
  156.2 5.7 %fusion.33 = (f32[640,10,1]{2,1,0:T(8,128)}, f32[640,10,1]{2,1,0:T(8,128)}) fusion(f32[640,10,128]{2,1,0:T(8,128)S(1)} %pad_maximum_fusion.3), kind=kLoop, calls=%fused_computation.70 | loop fusion | bytes 102400 | tf_op jit(solution)/shard_map/slice | solution.py:20
  161.9 3.3 %copy.41 = f32[640,10,1]{0,2,1:T(1,128)S(1)} copy(f32[640,10,1]{2,1,0:T(8,128)} %get-tuple-element.4) | data formatting | bytes 51200 | tf_op jit(solution)/shard_map/slice | solution.py:20
  165.3 3.3 %copy.42 = f32[640,10,1]{0,2,1:T(1,128)S(1)} copy(f32[640,10,1]{2,1,0:T(8,128)} %get-tuple-element.5) | data formatting | bytes 51200 | tf_op jit(solution)/shard_map/slice | solution.py:19
  168.6 4.8 %collective-permute-start.7 = (f32[640,10,1]{0,2,1:T(1,128)S(1)}, f32[640,10,1]{0,2,1:T(1,128)S(1)}, u32[]{:S(2)}, u32[]{:S(2)}) collective-permute-start(f32[640,10,1]{0,2,1:T(1,128)S(1)} %copy.42), channel_id=1, source_target_pairs={{8,0},{16,8},{24,16},{32,24},{40,32},{48,40},{56,48},{64,56},{72,6... | collective-permute-start | bytes 76808 | tf_op jit(solution)/shard_map/ppermute | solution.py:25
  173.4 3.2 %copy.43 = f32[640,10,1]{2,1,0:T(8,128)} copy(f32[640,10,1]{0,2,1:T(1,128)S(1)} %collective-permute-done.6) | data formatting | bytes 51200 | tf_op jit(solution)/shard_map/ppermute | solution.py:23
  176.6 3.2 %copy.44 = f32[640,10,1]{2,1,0:T(8,128)} copy(f32[640,10,1]{0,2,1:T(1,128)S(1)} %collective-permute-done.7) | data formatting | bytes 51200 | tf_op jit(solution)/shard_map/ppermute | solution.py:25
  179.8 10.8 %pad_maximum_fusion.1 = f32[640,10,130]{2,1,0:T(8,128)S(1)} fusion(f32[640,10,1]{2,1,0:T(8,128)} %copy.44, f32[640,1,128]{2,1,0:T(1,128)S(1)} %collective-permute-done.5, f32[640,8,128]{2,1,0:T(8,128)} %bitcast.43, f32[640,1,128]{2,1,0:T(1,128)S(1)} %collective-permute-done.4, f32[640,10,1]{2,1,0:T(8,128)} %copy.43), kind=kLoop, calls=%fused_computation.3 | loop fusion | flops 3328000 | bytes 6656000 | tf_op jit(solution)/shard_map/concatenate | solution.py:21
  190.6 0.6 slice.123
  191.2 0.7 slice.122
  192.6 1.9 copy-done.3
  194.6 16.4 %fusion.13 = f32[4,160,8,128]{3,2,1,0:T(8,128)} fusion(f32[4,160,8,128]{3,2,1,0:T(8,128)S(1)} %bitcast.49, f32[1,160,8,128]{3,2,1,0:T(8,128)S(1)} %bitcast.54, f32[4,160,10,130]{3,2,1,0:T(8,128)} %bitcast.40, f32[3,160,8,128]{3,2,1,0:T(8,128)S(1)} %slice.123, f32[8]{0:T(128)S(1)} %and_convert_fusion, f32[8,128]{1,0:T(8,128)S(1)} %copy-done.8), kind=kLoop, calls=%fused_computation.21 | loop fusion | flops 9830400 | bytes 20975648 | tf_op jit(solution)/shard_map/mul | solution.py:61
  (39 shorter events, 1.6 us)
Async XLA Ops:
  0.6 121.8 %copy-start = (bf16[1,32,128,128]{3,2,1,0:T(8,128)(2,1)S(1)}, bf16[1,32,128,128]{3,2,1,0:T(8,128)(2,1)}, u32[]{:S(2)}) copy-start(bf16[1,32,128,128]{3,2,1,0:T(8,128)(2,1)} %param.11) | copy-start | bytes 3145732
  31.9 15.0 %copy-start.9 = (s32[1,32,1]{1,2,0:T(1,128)S(1)}, s32[1,32,1]{1,2,0:T(1,128)}, u32[]{:S(2)}) copy-start(s32[1,32,1]{1,2,0:T(1,128)} %param.8) | copy-start | bytes 388
  31.9 88.0 %all-to-all-start.1 = ((bf16[64,160,128]{2,1,0:T(8,128)(2,1)}), bf16[64,160,128]{2,1,0:T(8,128)(2,1)}, u32[]{:S(2)}, u32[]{:S(2)}) async-start(bf16[64,160,128]{2,1,0:T(8,128)(2,1)} %broadcast_select_fusion), calls=%async_computation.1 | async-start | bytes 5242880 | tf_op jit(solution)/shard_map/all_to_all | solution.py:86
  39.8 9.1 %collective-permute-start = (f32[640,1,128]{2,1,0:T(1,128)S(1)}, f32[640,1,128]{2,1,0:T(1,128)S(1)}, u32[]{:S(2)}, u32[]{:S(2)}) collective-permute-start(f32[640,1,128]{2,1,0:T(1,128)S(1)} %get-tuple-element.14), channel_id=1, source_target_pairs={{0,1},{1,2},{2,3},{3,4},{4,5},{5,6},{6,7},{8,9},{9,10},{10,11},{11... | collective-permute-start | bytes 983048 | tf_op jit(solution)/shard_map/ppermute | solution.py:23
  45.0 8.8 %collective-permute-start.1 = (f32[640,1,128]{2,1,0:T(1,128)S(1)}, f32[640,1,128]{2,1,0:T(1,128)S(1)}, u32[]{:S(2)}, u32[]{:S(2)}) collective-permute-start(f32[640,1,128]{2,1,0:T(1,128)S(1)} %get-tuple-element.15), channel_id=1, source_target_pairs={{1,0},{2,1},{3,2},{4,3},{5,4},{6,5},{7,6},{9,8},{10,9},{11,10},{12... | collective-permute-start | bytes 983048 | tf_op jit(solution)/shard_map/ppermute | solution.py:25
  68.7 29.8 %collective-permute-start.3 = (f32[640,10,1]{0,2,1:T(1,128)S(1)}, f32[640,10,1]{0,2,1:T(1,128)S(1)}, u32[]{:S(2)}, u32[]{:S(2)}) collective-permute-start(f32[640,10,1]{0,2,1:T(1,128)S(1)} %copy.38), channel_id=1, source_target_pairs={{8,0},{16,8},{24,16},{32,24},{40,32},{48,40},{56,48},{64,56},{72,6... | collective-permute-start | bytes 76808 | tf_op jit(solution)/shard_map/ppermute | solution.py:25
  73.6 21.7 %collective-permute-start.2 = (f32[640,10,1]{0,2,1:T(1,128)S(1)}, f32[640,10,1]{0,2,1:T(1,128)S(1)}, u32[]{:S(2)}, u32[]{:S(2)}) collective-permute-start(f32[640,10,1]{0,2,1:T(1,128)S(1)} %copy.37), channel_id=1, source_target_pairs={{0,8},{8,16},{16,24},{24,32},{32,40},{40,48},{48,56},{56,64},{64,7... | collective-permute-start | bytes 76808 | tf_op jit(solution)/shard_map/ppermute | solution.py:23
  112.4 4.6 %copy-start.2 = (f32[640,10,130]{2,1,0:T(8,128)}, f32[640,10,130]{2,1,0:T(8,128)S(1)}, u32[]{:S(2)}) copy-start(f32[640,10,130]{2,1,0:T(8,128)S(1)} %pad_maximum_fusion) | copy-start | bytes 9984004
  122.4 0.7 copy-start.10
  123.0 2.5 %copy-start.5 = (f32[4,5,16,2,8,128]{5,4,3,2,1,0:T(8,128)S(1)}, f32[4,5,16,2,8,128]{5,4,3,2,1,0:T(8,128)}, u32[]{:S(2)}) copy-start(f32[4,5,16,2,8,128]{5,4,3,2,1,0:T(8,128)} %maximum_multiply_fusion) | copy-start | bytes 7864324
  123.0 2.5 %copy-start.8 = (f32[8,128]{1,0:T(8,128)S(1)}, f32[8,128]{1,0:T(8,128)}, u32[]{:S(2)}) copy-start(f32[8,128]{1,0:T(8,128)} %param.13) | copy-start | bytes 12292
  125.5 15.9 %copy-start.6 = (f32[160,128,8]{1,2,0:T(8,128)}, f32[160,128,8]{1,2,0:T(8,128)S(1)}, u32[]{:S(2)}) copy-start(f32[160,128,8]{1,2,0:T(8,128)S(1)} %fusion.18) | copy-start | bytes 1966084
  141.4 14.8 %copy-start.4 = (f32[4,160,8,128]{3,2,1,0:T(8,128)}, f32[4,160,8,128]{3,2,1,0:T(8,128)S(1)}, u32[]{:S(2)}) copy-start(f32[4,160,8,128]{3,2,1,0:T(8,128)S(1)} %fusion.6) | copy-start | bytes 7864324
  141.9 9.0 %collective-permute-start.4 = (f32[640,1,128]{2,1,0:T(1,128)S(1)}, f32[640,1,128]{2,1,0:T(1,128)S(1)}, u32[]{:S(2)}, u32[]{:S(2)}) collective-permute-start(f32[640,1,128]{2,1,0:T(1,128)S(1)} %get-tuple-element.10), channel_id=1, source_target_pairs={{0,1},{1,2},{2,3},{3,4},{4,5},{5,6},{6,7},{8,9},{9,10},{10,11},{11... | collective-permute-start | bytes 983048 | tf_op jit(solution)/shard_map/ppermute | solution.py:23
  146.8 8.4 %collective-permute-start.5 = (f32[640,1,128]{2,1,0:T(1,128)S(1)}, f32[640,1,128]{2,1,0:T(1,128)S(1)}, u32[]{:S(2)}, u32[]{:S(2)}) collective-permute-start(f32[640,1,128]{2,1,0:T(1,128)S(1)} %get-tuple-element.11), channel_id=1, source_target_pairs={{1,0},{2,1},{3,2},{4,3},{5,4},{6,5},{7,6},{9,8},{10,9},{11,10},{12... | collective-permute-start | bytes 983048 | tf_op jit(solution)/shard_map/ppermute | solution.py:25
  165.2 8.2 %collective-permute-start.6 = (f32[640,10,1]{0,2,1:T(1,128)S(1)}, f32[640,10,1]{0,2,1:T(1,128)S(1)}, u32[]{:S(2)}, u32[]{:S(2)}) collective-permute-start(f32[640,10,1]{0,2,1:T(1,128)S(1)} %copy.41), channel_id=1, source_target_pairs={{0,8},{8,16},{16,24},{24,32},{32,40},{40,48},{48,56},{56,64},{64,7... | collective-permute-start | bytes 76808 | tf_op jit(solution)/shard_map/ppermute | solution.py:23
  168.6 8.0 %collective-permute-start.7 = (f32[640,10,1]{0,2,1:T(1,128)S(1)}, f32[640,10,1]{0,2,1:T(1,128)S(1)}, u32[]{:S(2)}, u32[]{:S(2)}) collective-permute-start(f32[640,10,1]{0,2,1:T(1,128)S(1)} %copy.42), channel_id=1, source_target_pairs={{8,0},{16,8},{24,16},{32,24},{40,32},{48,40},{56,48},{64,56},{72,6... | collective-permute-start | bytes 76808 | tf_op jit(solution)/shard_map/ppermute | solution.py:25
  190.6 4.0 %copy-start.3 = (f32[640,10,130]{2,1,0:T(8,128)}, f32[640,10,130]{2,1,0:T(8,128)S(1)}, u32[]{:S(2)}) copy-start(f32[640,10,130]{2,1,0:T(8,128)S(1)} %pad_maximum_fusion.1) | copy-start | bytes 9984004
  192.3 2.3 %copy-start.7 = (f32[160,128,8]{1,2,0:T(8,128)S(1)}, f32[160,128,8]{1,2,0:T(8,128)}, u32[]{:S(2)}) copy-start(f32[160,128,8]{1,2,0:T(8,128)} %copy-done.6) | copy-start | bytes 1966084
  194.6 16.4 %copy-start.1 = (bf16[1,32,128,128]{3,2,1,0:T(8,128)(2,1)S(1)}, bf16[1,32,128,128]{3,2,1,0:T(8,128)(2,1)}, u32[]{:S(2)}) copy-start(bf16[1,32,128,128]{3,2,1,0:T(8,128)(2,1)} %param.11) | copy-start | bytes 3145732
where the time goes:
time: 212 us; the launch traced here: 211 us
  other arithmetic  67 us (32%)
  local copies, waits for them, and re-layouts  56 us (26%)
  waiting for transfers between devices  34.7 us (16%)
  starting transfers between devices  28.9 us (14%)
  blocking collectives  20.4 us (10%)
  matrix products  2.98 us (1%)
    mul x2, other arithmetic, advance(): return updated * inside[None, None, :, None]  32.3 us
    ppermute x4, waiting for transfers between devices, padded_2(): lax.ppermute(tail, axis, [(i, (i + 1) % count) for i in range(ends)])  25.5 us
    concatenate x4, other arithmetic, padded_2(): jnp.concatenate([lax.ppermute(tail, axis, [(i, (i + 1) % count) for i in...  25.2 us
    slice x6, local copies, waits for them, and re-layouts, padded_2(): lax.slice_in_dim(cells, cells.shape[dim] - width, cells.shape[dim], axis=...  21.3 us
    all_to_all x1, blocking collectives, per_device(): lax.all_to_all(wanted, 'rows', split_axis=0, concat_axis=0, tiled=True)  20.4 us
    ppermute x4, starting transfers between devices, padded_2(): lax.ppermute(head, axis, [((i + 1) % count, i) for i in range(ends)])  13.8 us
    ppermute x4, starting transfers between devices, padded_2(): lax.ppermute(tail, axis, [(i, (i + 1) % count) for i in range(ends)])  10.2 us
    ppermute x4, waiting for transfers between devices, padded_2(): lax.ppermute(head, axis, [((i + 1) % count, i) for i in range(ends)])  9.2 us
  transfers between devices with their start and end apart: 9, of which 5 were waited for; matrix products, arithmetic and copies ran while one was open for 22% of the time, Pallas kernels for 0%

commit v1 on v0

v1 whole, which is shorter than its diff:
```python
import functools

import jax
import jax.numpy as jnp
from jax import lax
from jax.experimental import pallas as pl
from jax.experimental.pallas import tpu as pltpu
from jax.sharding import PartitionSpec as P

NVAR = 5
UPWIND = 0.45
DIFFUSE = 0.2
TURNING = 0.02
NY = 4
NZ = 8
CAP = 2
GROUP = 32
VMEM = pl.BlockSpec(memory_space=pltpu.VMEM)
SMEM = pl.BlockSpec(memory_space=pltpu.SMEM)
STAGES = ((0, -1, 1, -2, 2, -3, 3, 4),)


def rows8(start):
    return pl.ds(pl.multiple_of(start, 8), 8)


def pack_edges(tiles, lane4):
    packed = jnp.zeros((8, 128), jnp.float32)
    for c, tile in enumerate(tiles):
        packed = jnp.where(lane4 == c, pltpu.roll(tile, 4 * c + 1, 1), packed)
    return packed


def edges_kernel(v_ref, packed_ref, top_ref, bottom_ref):
    coefs = top_ref.shape[0]
    lane4 = lax.broadcasted_iota(jnp.int32, (8, 128), 1) // 4
    top_ref[...] = v_ref[pl.ds(0, coefs, stride=8), :]
    bottom_ref[...] = v_ref[pl.ds(7, coefs, stride=8), :]

    def body(i, carry):
        base = i * (GROUP * 8)
        tiles = [v_ref[rows8(base + 8 * c), :] for c in range(GROUP)]
        packed_ref[i] = pack_edges(tiles, lane4)
        return carry

    lax.fori_loop(0, coefs // GROUP, body, 0)


def combine_halo(left, right, lane):
    return jnp.where(lane % 4 == 1, pltpu.roll(left, 1, 1), pltpu.roll(right, 127, 1))


def operator_pair(x0, x1, s0, s1, h, c, k, diag, row, lane):
    out = []
    for j, (x, s) in enumerate(((x0, s0), (x1, s1))):
        edge = pltpu.roll(h, (128 - (4 * (c + j) + 1)) % 128, 1)
        above = jnp.where(row == 0, s, pltpu.roll(x, 1, 0))
        below = jnp.where(row == 7, s, pltpu.roll(x, 7, 0))
        left = jnp.where(lane == 0, edge, pltpu.roll(x, 1, 1))
        right = jnp.where(lane == 127, edge, pltpu.roll(x, 127, 1))
        beside = (above + below) + (left + right)
        turn = (TURNING * k) * x1 if j == 0 else (-TURNING * k) * x0
        out.append(diag * x + DIFFUSE * beside + turn)
    return out


def section_kernel(with_edges, v_ref, top_ref, bottom_ref, left_ref, right_ref, damp_ref, out_ref, *rest):
    if with_edges:
        packed_ref, new_top_ref, new_bottom_ref, halo = rest
    else:
        (halo,) = rest
    coefs = top_ref.shape[0]
    groups = coefs // GROUP
    row = lax.broadcasted_iota(jnp.int32, (8, 128), 0)
    lane = lax.broadcasted_iota(jnp.int32, (8, 128), 1)
    halo[pl.ds(0, coefs, stride=8), :] = top_ref[...]
    halo[pl.ds(7, coefs, stride=8), :] = bottom_ref[...]
    diag = (1.0 - UPWIND - 4.0 * DIFFUSE) - damp_ref[...]

    def body(i, carry):
        base = i * (GROUP * 8)
        behind = jnp.maximum(i - NVAR, 0) * (GROUP * 8)
        upwind = jnp.where(i >= NVAR, UPWIND, 0.0).astype(jnp.float32)
        h = combine_halo(left_ref[i], right_ref[i], lane)
        packed = jnp.zeros((8, 128), jnp.float32)
        for c in range(0, GROUP, 2):
            at = [rows8(base + 8 * (c + j)) for j in range(2)]
            new = operator_pair(
                v_ref[at[0], :], v_ref[at[1], :], halo[at[0], :], halo[at[1], :],
                h, c, float(c // 2 + 1), diag, row, lane,
            )
            for j in range(2):
                tile = new[j] + upwind * v_ref[rows8(behind + 8 * (c + j)), :]
                out_ref[at[j], :] = tile
                if with_edges:
                    packed = jnp.where(lane // 4 == c + j, pltpu.roll(tile, 4 * (c + j) + 1, 1), packed)
        if with_edges:
            packed_ref[i] = packed
        return carry

    lax.fori_loop(0, groups, body, 0)
    if with_edges:
        new_top_ref[...] = out_ref[pl.ds(0, coefs, stride=8), :]
        new_bottom_ref[...] = out_ref[pl.ds(7, coefs, stride=8), :]


def finish_kernel(face_ref, top_ref, bottom_ref, left_ref, right_ref, damp_ref, part_ref, out_ref, halo):
    coefs = top_ref.shape[0]
    row = lax.broadcasted_iota(jnp.int32, (8, 128), 0)
    lane = lax.broadcasted_iota(jnp.int32, (8, 128), 1)
    halo[pl.ds(0, coefs, stride=8), :] = top_ref[...]
    halo[pl.ds(7, coefs, stride=8), :] = bottom_ref[...]
    diag = (2.0 - UPWIND - 4.0 * DIFFUSE) - damp_ref[...]

    def body(i, carry):
        base = i * (GROUP * 8)
        h = combine_halo(left_ref[i], right_ref[i], lane)
        for c in range(0, GROUP, 2):
            at = [rows8(base + 8 * (c + j)) for j in range(2)]
            x = [face_ref[a, :] for a in at]
            new = operator_pair(
                x[0], x[1], halo[at[0], :], halo[at[1], :], h, c, float(c // 2 + 1), diag, row, lane
            )
            for j in range(2):
                out_ref[at[j], :] = part_ref[at[j], :] + UPWIND * new[j]
                nxt = rows8(coefs * 8 + base + 8 * (c + j))
                out_ref[nxt, :] = part_ref[nxt, :] + (UPWIND * UPWIND) * x[j]
        return carry

    lax.fori_loop(0, coefs // GROUP, body, 0)


def plan_kernel(where_ref, own_ref, near_ref, far_ref, back_ref, send_ref, slot_ref, count):
    my_z = where_ref[0]
    my_y = where_ref[1]

    def clear(i, carry):
        send_ref[i] = 0
        return carry

    lax.fori_loop(0, NY * NZ * CAP, clear, 0)
    for shift, asked in enumerate((own_ref, near_ref, far_ref, back_ref)):
        peer = (my_y + shift) % NY

        def zero(i, carry):
            count[i] = 0
            return carry

        lax.fori_loop(0, NZ * NY, zero, 0)

        def pair(p, carry, asked=asked, peer=peer, shift=shift):
            source = asked[0, p]
            rank = jnp.minimum(count[source], CAP - 1)
            count[source] = rank + 1
            distance = (source // NY - my_z + NZ) % NZ

            @pl.when(source % NY == my_y)
            def _():
                send_ref[(peer * NZ + distance) * CAP + rank] = asked[1, p]

            if shift == 0:
                slot_ref[p] = ((source % NY) * NZ + distance) * CAP + rank
            return carry

        lax.fori_loop(0, asked.shape[1], pair, 0)


def select_kernel(stage, send_ref, *refs):
    out_ref = refs[-1]
    half = refs[0].shape[1]
    for peer in range(NY):
        for i, distance in enumerate(stage):
            for rank in range(CAP):
                block = send_ref[(peer * NZ + distance % NZ) * CAP + rank]
                slot = (peer * len(stage) + i) * CAP + rank
                out_ref[slot, :half] = refs[2 * i][block]
                out_ref[slot, half:] = refs[2 * i + 1][block]


def face_kernel(stage, slot_ref, row_ref, came_ref, weight_ref, face_ref, packed_ref, top_ref, bottom_ref, total):
    coefs = top_ref.shape[0]
    lane4 = lax.broadcasted_iota(jnp.int32, (8, 128), 1) // 4
    total[...] = jnp.zeros_like(total)
    place = {d % NZ: i for i, d in enumerate(stage)}
    for p in range(weight_ref.shape[0]):
        slot = slot_ref[p]
        distance = (slot // CAP) % NZ
        spot = jnp.int32(0)
        for d, i in place.items():
            spot = jnp.where(distance == d, i, spot)
        at = ((slot // (CAP * NZ)) * len(stage) + spot) * CAP + slot % CAP
        term = jnp.dot(came_ref[at], weight_ref[p], preferred_element_type=jnp.float32)
        total[row_ref[p]] += term
    for r in range(8):
        face_ref[pl.ds(r, coefs, stride=8), :] = total[r]
    top_ref[...] = total[0]
    bottom_ref[...] = total[7]

    def body(i, carry):
        tiles = [face_ref[rows8(i * (GROUP * 8) + 8 * c), :] for c in range(GROUP)]
        packed_ref[i] = pack_edges(tiles, lane4)
        return carry

    lax.fori_loop(0, coefs // GROUP, body, 0)


def f32(*shape):
    return jax.ShapeDtypeStruct(shape, jnp.float32)


def per_device(rotor_face, pair_source, pair_block, pair_row, pair_weight, stator_field, damping):
    coefs, width = rotor_face.shape[2:]
    layers = stator_field.shape[0]
    pairs = pair_block.shape[1]
    every = layers * coefs
    groups = every // GROUP
    n_span = lax.axis_size("span")
    n_rows = lax.axis_size("rows")
    me = lax.axis_index("rows")
    where = jnp.stack([me // NY, me % NY])

    def up_z(k):
        return [(i, (i // NY + k) % NZ * NY + i % NY) for i in range(n_rows)]

    def up_y(k):
        return [(i, i // NY * NY + (i % NY + k) % NY) for i in range(n_rows)]

    def halos(packed, top, bottom):
        left = lax.ppermute(packed, "rows", [(i, (i + 1) % n_rows) for i in range(n_rows)])
        right = lax.ppermute(packed, "rows", [((i + 1) % n_rows, i) for i in range(n_rows)])
        above = lax.ppermute(bottom, "span", [(i, i + 1) for i in range(n_span - 1)])
        below = lax.ppermute(top, "span", [(i + 1, i) for i in range(n_span - 1)])
        return above, below, left, right

    wanted = jnp.stack([pair_source[0, :, 0], pair_block[0]])
    asked = [wanted] + [lax.ppermute(wanted, "rows", up_y(-k)) for k in range(1, NY)]
    half = coefs // 2
    own = rotor_face[0]
    held = {0: [own[:, :half], own[:, half:]]}
    for k in range(1, NZ // 2):
        held[-k] = [lax.ppermute(held[1 - k][j], "rows", up_z(1)) for j in range(2)]
        held[k] = [lax.ppermute(held[k - 1][j], "rows", up_z(-1)) for j in range(2)]
    last = NZ // 2 - 1
    held[NZ // 2] = [
        lax.ppermute(held[-last][0], "rows", up_z(1)),
        lax.ppermute(held[last][1], "rows", up_z(-1)),
    ]

    send_table, slot_of = pl.pallas_call(
        plan_kernel,
        out_shape=(
            jax.ShapeDtypeStruct((NY * NZ * CAP,), jnp.int32),
            jax.ShapeDtypeStruct((pairs,), jnp.int32),
        ),
        in_specs=[SMEM] * 5,
        out_specs=(SMEM, SMEM),
        scratch_shapes=[pltpu.SMEM((NZ * NY,), jnp.int32)],
        name="plan",
    )(where, *asked)

    flat = stator_field.reshape(every * 8, width)
    packed, top, bottom = pl.pallas_call(
        edges_kernel,
        out_shape=(f32(groups, 8, 128), f32(every, width), f32(every, width)),
        in_specs=[VMEM],
        out_specs=(VMEM,) * 3,
        name="edges",
    )(flat)
    first, packed, top, bottom = pl.pallas_call(
        functools.partial(section_kernel, True),
        out_shape=(f32(every * 8, width), f32(groups, 8, 128), f32(every, width), f32(every, width)),
        in_specs=[VMEM] * 6,
        out_specs=(VMEM,) * 4,
        scratch_shapes=[pltpu.VMEM((every * 8, width), jnp.float32)],
        name="section_one",
    )(flat, *halos(packed, top, bottom), damping)
    second = pl.pallas_call(
        functools.partial(section_kernel, False),
        out_shape=f32(every * 8, width),
        in_specs=[VMEM] * 6,
        out_specs=VMEM,
        scratch_shapes=[pltpu.VMEM((every * 8, width), jnp.float32)],
        name="section_two",
    )(first, *halos(packed, top, bottom), damping)

    stage = STAGES[0]
    slots = NY * len(stage) * CAP
    sent = pl.pallas_call(
        functools.partial(select_kernel, stage),
        out_shape=jax.ShapeDtypeStruct((slots, coefs, width), jnp.bfloat16),
        in_specs=[SMEM] + [VMEM] * (2 * len(stage)),
        out_specs=VMEM,
        name="select",
    )(send_table, *(held[d][j] for d in stage for j in range(2)))
    same_z = [[z * NY + y for y in range(NY)] for z in range(NZ)]
    came = lax.all_to_all(sent, "rows", split_axis=0, concat_axis=0, tiled=True, axis_index_groups=same_z)
    face, packed, top, bottom = pl.pallas_call(
        functools.partial(face_kernel, stage),
        out_shape=(f32(coefs * 8, width), f32(coefs // GROUP, 8, 128), f32(coefs, width), f32(coefs, width)),
        in_specs=[SMEM, SMEM, VMEM, VMEM],
        out_specs=(VMEM,) * 4,
        scratch_shapes=[pltpu.VMEM((8, coefs, width), jnp.float32)],
        name="face",
    )(slot_of, pair_row[0], came, pair_weight[0])

    two = pl.BlockSpec((2 * coefs * 8, width), lambda i: (0, 0))
    updated = pl.pallas_call(
        finish_kernel,
        grid=(1,),
        out_shape=f32(every * 8, width),
        in_specs=[VMEM] * 6 + [two],
        out_specs=two,
        scratch_shapes=[pltpu.VMEM((coefs * 8, width), jnp.float32)],
        input_output_aliases={6: 0},
        name="finish",
    )(face, *halos(packed, top, bottom), damping, second)
    return face.reshape(coefs, 8, width), updated.reshape(stator_field.shape)


def solution(mesh):
    placed = (
        P("span", "rows", None, None),
        P("span", "rows", None),
        P("span", "rows"),
        P("span", "rows"),
        P("span", "rows", None, None),
        P(None, None, "span", "rows"),
        P("span", "rows"),
    )
    return jax.shard_map(
        per_device,
        mesh=mesh,
        in_specs=placed,
        out_specs=(P(None, "span", "rows"), P(None, None, "span", "rows")),
        check_vma=False,
    )
```

time: 212 us -> 136 us (0.64)
  other arithmetic: 67 us -> 1.23 us
  local copies, waits for them, and re-layouts: 56 us -> 6.69 us
  starting transfers between devices: 28.9 us -> 68.7 us
  Pallas kernels: 0 us -> 37.8 us
  blocking collectives: 20.4 us -> 0 us
  waiting for transfers between devices: 34.7 us -> 20.2 us
  matrix products: 2.98 us -> 0 us
    ppermute x8 -> x29, starting transfers between devices: 24 us -> 64.8 us  [the longest x3 22.2 us: halos(): lax.ppermute(bottom, 'span', [(i, i + 1) for i in range(n_span - 1)])]
    pallas_call x0 -> x7, Pallas kernels: none -> 37.8 us  [the longest x1 9.16 us: per_device(): pl.pallas_call(functools.partial(section_kernel, True), out_shape=(f32(ev...]
    mul x6 -> x0, other arithmetic: 35.2 us -> none  [the longest x2 32.3 us: advance(): return updated * inside[None, None, :, None]]
    slice x12 -> x1, local copies, waits for them, and re-layouts: 32.2 us -> 1.02 us  [per_device(): held = {0: [own[:, :half], own[:, half:]]}]
    concatenate x4 -> x0, other arithmetic: 25.2 us -> none  [padded_2(): jnp.concatenate([lax.ppermute(tail, axis, [(i, (i + 1) % count) for i in...]
    all_to_all x1 -> x0, blocking collectives: 20.4 us -> none  [per_device(): lax.all_to_all(wanted, 'rows', split_axis=0, concat_axis=0, tiled=True)]
    ppermute x8 -> x29, waiting for transfers between devices: 34.7 us -> 20.2 us  [the longest x6 6.74 us: per_device(): held[-k] = [lax.ppermute(held[1 - k][j], 'rows', up_z(1)) for j in range(2)]]
    ppermute x4 -> x0, local copies, waits for them, and re-layouts: 12.7 us -> none  [the longest x2 6.4 us: padded_2(): lax.ppermute(tail, axis, [(i, (i + 1) % count) for i in range(ends)])]
  transfers between devices with their start and end apart: 9 -> 30, of which waited for: 5 -> 9; matrix products, arithmetic and copies ran while one was open for 22% -> 1% of each run, Pallas kernels for 0% -> 23%
where the time goes in v1:
time: 136 us
  starting transfers between devices  68.7 us (51%)
  Pallas kernels  37.8 us (28%)
  waiting for transfers between devices  20.2 us (15%)
  local copies, waits for them, and re-layouts  6.69 us (5%)
    ppermute x3, starting transfers between devices, halos(): lax.ppermute(bottom, 'span', [(i, i + 1) for i in range(n_span - 1)])  22.2 us
    ppermute x6, starting transfers between devices, per_device(): held[k] = [lax.ppermute(held[k - 1][j], 'rows', up_z(-1)) for j in range(2)]  18.1 us
    ppermute x3, starting transfers between devices, halos(): lax.ppermute(packed, 'rows', [((i + 1) % n_rows, i) for i in range(n_rows)])  11.9 us
    pallas_call x1, Pallas kernels, per_device(): pl.pallas_call(functools.partial(section_kernel, True), out_shape=(f32(ev...  9.16 us
    pallas_call x1, Pallas kernels, per_device(): pl.pallas_call(functools.partial(section_kernel, False), out_shape=f32(ev...  7.65 us
    ppermute x6, waiting for transfers between devices, per_device(): held[-k] = [lax.ppermute(held[1 - k][j], 'rows', up_z(1)) for j in range(2)]  6.74 us
    ppermute x3, waiting for transfers between devices, halos(): lax.ppermute(packed, 'rows', [(i, (i + 1) % n_rows) for i in range(n_rows)])  6.05 us
    ppermute x3, starting transfers between devices, halos(): below = lax.ppermute(top, 'span', [(i + 1, i) for i in range(n_span - 1)])  5.76 us
  transfers between devices with their start and end apart: 30, of which 9 were waited for; matrix products, arithmetic and copies ran while one was open for 1% of the time, Pallas kernels for 23%

profile of v1, /device:TPU:1, one launch (start us, length us, event | category | flops | bytes accessed | tf_op | source)
XLA Modules:
  0.0 135.8 jit_solution(1782906925054893394)
XLA Ops:
  0.6 1.0 fusion
  1.7 6.5 %collective-permute-start.6 = (bf16[8,80,128]{2,1,0:T(8,128)(2,1)S(1)}, bf16[8,80,128]{2,1,0:T(8,128)(2,1)S(1)}, u32[]{:S(2)}, u32[]{:S(2)}) collective-permute-start(bf16[8,80,128]{2,1,0:T(8,128)(2,1)S(1)} %get-tuple-element.28.refs_1_), channel_id=1, source_target_pairs={{0,224},{8,232},{16,240},{24,248},{32,0},{40,8},{48,16},{56,24},{6... | collective-permute-start | bytes 491528 | tf_op jit(solution)/shard_map/ppermute | solution.py:242
  8.2 2.7 %collective-permute-start.5 = (bf16[8,80,128]{2,1,0:T(8,128)(2,1)S(1)}, bf16[8,80,128]{2,1,0:T(8,128)(2,1)S(1)}, u32[]{:S(2)}, u32[]{:S(2)}) collective-permute-start(bf16[8,80,128]{2,1,0:T(8,128)(2,1)S(1)} %get-tuple-element.29.refs_0_), channel_id=1, source_target_pairs={{0,224},{8,232},{16,240},{24,248},{32,0},{40,8},{48,16},{56,24},{6... | collective-permute-start | bytes 491528 | tf_op jit(solution)/shard_map/ppermute | solution.py:242
  10.8 0.2 collective-permute-done.6.refs_5_
  11.0 3.4 %collective-permute-start.10 = (bf16[8,80,128]{2,1,0:T(8,128)(2,1)S(1)}, bf16[8,80,128]{2,1,0:T(8,128)(2,1)S(1)}, u32[]{:S(2)}, u32[]{:S(2)}) collective-permute-start(bf16[8,80,128]{2,1,0:T(8,128)(2,1)S(1)} %collective-permute-done.6.refs_5_), channel_id=1, source_target_pairs={{0,224},{8,232},{16,240},{24,248},{32,0},{40,8},{48,16},{56,24},{6... | collective-permute-start | bytes 491528 | tf_op jit(solution)/shard_map/ppermute | solution.py:242
  14.5 3.2 %collective-permute-done.4.refs_3_ = bf16[8,80,128]{2,1,0:T(8,128)(2,1)S(1)} collective-permute-done((bf16[8,80,128]{2,1,0:T(8,128)(2,1)S(1)}, bf16[8,80,128]{2,1,0:T(8,128)(2,1)S(1)}, u32[]{:S(2)}, u32[]{:S(2)}) %collective-permute-start.4) | collective-permute-done | bytes 163872 | tf_op jit(solution)/shard_map/ppermute | solution.py:241
  17.7 2.7 %collective-permute-start.9 = (bf16[8,80,128]{2,1,0:T(8,128)(2,1)S(1)}, bf16[8,80,128]{2,1,0:T(8,128)(2,1)S(1)}, u32[]{:S(2)}, u32[]{:S(2)}) collective-permute-start(bf16[8,80,128]{2,1,0:T(8,128)(2,1)S(1)} %collective-permute-done.5.refs_4_), channel_id=1, source_target_pairs={{0,224},{8,232},{16,240},{24,248},{32,0},{40,8},{48,16},{56,24},{6... | collective-permute-start | bytes 491528 | tf_op jit(solution)/shard_map/ppermute | solution.py:242
  20.4 0.2 collective-permute-start.14
  20.6 1.3 collective-permute-start.11
  21.8 3.1 %collective-permute-done.8.refs_7_ = bf16[8,80,128]{2,1,0:T(8,128)(2,1)S(1)} collective-permute-done((bf16[8,80,128]{2,1,0:T(8,128)(2,1)S(1)}, bf16[8,80,128]{2,1,0:T(8,128)(2,1)S(1)}, u32[]{:S(2)}, u32[]{:S(2)}) %collective-permute-start.8) | collective-permute-done | bytes 163872 | tf_op jit(solution)/shard_map/ppermute | solution.py:241
  25.0 2.7 %collective-permute-start.13 = (bf16[8,80,128]{2,1,0:T(8,128)(2,1)S(1)}, bf16[8,80,128]{2,1,0:T(8,128)(2,1)S(1)}, u32[]{:S(2)}, u32[]{:S(2)}) collective-permute-start(bf16[8,80,128]{2,1,0:T(8,128)(2,1)S(1)} %collective-permute-done.9.refs_8_), channel_id=1, source_target_pairs={{0,224},{8,232},{16,240},{24,248},{32,0},{40,8},{48,16},{56,24},{6... | collective-permute-start | bytes 491528 | tf_op jit(solution)/shard_map/ppermute | solution.py:242
  27.6 0.4 collective-permute-start.16
  28.0 0.4 collective-permute-done.11.refs_10_
  28.5 0.7 collective-permute-start.15
  29.1 0.7 pad_add_fusion.own_ref
  29.8 1.4 %collective-permute-start.2 = (s32[2,32]{1,0:T(2,128)S(1)}, s32[2,32]{1,0:T(2,128)S(1)}, u32[]{:S(2)}, u32[]{:S(2)}) collective-permute-start(s32[2,32]{1,0:T(2,128)S(1)} %pad_add_fusion.own_ref), channel_id=1, source_target_pairs={{0,8},{8,16},{16,24},{24,0},{32,40},{40,48},{48,56},{56,32},{64,72... | collective-permute-start | bytes 776 | tf_op jit(solution)/shard_map/ppermute | solution.py:236
  31.2 2.7 %collective-permute-done.2.back_ref = s32[2,32]{1,0:T(2,128)S(1)} collective-permute-done((s32[2,32]{1,0:T(2,128)S(1)}, s32[2,32]{1,0:T(2,128)S(1)}, u32[]{:S(2)}, u32[]{:S(2)}) %collective-permute-start.2) | collective-permute-done | bytes 288 | tf_op jit(solution)/shard_map/ppermute | solution.py:236
  33.9 1.6 %collective-permute-start.1 = (s32[2,32]{1,0:T(2,128)S(1)}, s32[2,32]{1,0:T(2,128)S(1)}, u32[]{:S(2)}, u32[]{:S(2)}) collective-permute-start(s32[2,32]{1,0:T(2,128)S(1)} %pad_add_fusion.own_ref), channel_id=1, source_target_pairs={{0,16},{8,24},{16,0},{24,8},{32,48},{40,56},{48,32},{56,40},{64,80... | collective-permute-start | bytes 776 | tf_op jit(solution)/shard_map/ppermute | solution.py:236
  35.5 2.3 %collective-permute-done.1.far_ref = s32[2,32]{1,0:T(2,128)S(1)} collective-permute-done((s32[2,32]{1,0:T(2,128)S(1)}, s32[2,32]{1,0:T(2,128)S(1)}, u32[]{:S(2)}, u32[]{:S(2)}) %collective-permute-start.1) | collective-permute-done | bytes 288 | tf_op jit(solution)/shard_map/ppermute | solution.py:236
  37.8 1.5 %collective-permute-start = (s32[2,32]{1,0:T(2,128)S(1)}, s32[2,32]{1,0:T(2,128)S(1)}, u32[]{:S(2)}, u32[]{:S(2)}) collective-permute-start(s32[2,32]{1,0:T(2,128)S(1)} %pad_add_fusion.own_ref), channel_id=1, source_target_pairs={{0,24},{8,0},{16,8},{24,16},{32,56},{40,32},{48,40},{56,48},{64,88... | collective-permute-start | bytes 776 | tf_op jit(solution)/shard_map/ppermute | solution.py:236
  39.3 0.6 pad_add_fusion.1.where_ref
  39.8 0.4 collective-permute-done.near_ref
  40.2 0.5 copy-done.32
  40.8 4.9 %plan.1 = (s32[64]{0:T(128)}, s32[32]{0:T(128)}) custom-call(s32[2]{0:T(128)} %pad_add_fusion.1.where_ref, s32[2,32]{1,0:T(2,128)} %copy-done.29, s32[2,32]{1,0:T(2,128)} %copy-done.32, s32[2,32]{1,0:T(2,128)} %copy-done.31, s32[2,32]{1,0:T(2,128)} %copy-done.30), custom_call_target="tpu_custom_call" | custom-call | tf_op jit(solution)/shard_map/plan/pallas_call | solution.py:249
  45.8 0.5 copy-done.17
  46.5 3.5 %select.7 = bf16[64,160,128]{2,1,0:T(8,128)(2,1)} custom-call(s32[64]{0:T(128)} %get-tuple-element.16.send_ref, bf16[8,80,128]{2,1,0:T(8,128)(2,1)} %copy-done.2, bf16[8,80,128]{2,1,0:T(8,128)(2,1)} %copy-done.1, bf16[8,80,128]{2,1,0:T(8,128)(2,1)} %copy-done.8, bf16[8,80,128]{2,1,0:T(8,128)(2,1)} %copy-done.9, bf16[8,80,128]{2,1,0:T(8,128)(2,1)} %copy-done.10, ...), custom_call_target="tpu_custom_call" | custom-call | tf_op jit(solution)/shard_map/select/pallas_call | solution.py:288
  50.0 3.9 %all-to-all-start = ((bf16[64,160,128]{2,1,0:T(8,128)(2,1)}), bf16[64,160,128]{2,1,0:T(8,128)(2,1)S(1)}, u32[]{:S(2)}, u32[]{:S(2)}) async-start(bf16[64,160,128]{2,1,0:T(8,128)(2,1)} %select.7), calls=%async_computation | async-start | bytes 5242880 | tf_op jit(solution)/shard_map/all_to_all | solution.py:296
  53.9 4.7 %edges.1 = (f32[20,8,128]{2,1,0:T(8,128)}, f32[640,128]{1,0:T(8,128)}, f32[640,128]{1,0:T(8,128)}) custom-call(f32[5120,128]{1,0:T(8,128)} %bitcast.9), custom_call_target="tpu_custom_call" | custom-call | tf_op jit(solution)/shard_map/edges/pallas_call | solution.py:262
  58.6 11.6 %collective-permute-start.21 = (f32[640,128]{1,0:T(8,128)}, f32[640,128]{1,0:T(8,128)S(1)}, u32[]{:S(2)}, u32[]{:S(2)}) collective-permute-start(f32[640,128]{1,0:T(8,128)} %get-tuple-element.21), channel_id=1, source_target_pairs={{0,1},{1,2},{2,3},{3,4},{4,5},{5,6},{6,7},{8,9},{9,10},{10,11},{11... | collective-permute-start | bytes 983048 | tf_op jit(solution)/shard_map/ppermute | solution.py:231
  70.2 1.9 %collective-permute-start.22 = (f32[640,128]{1,0:T(8,128)}, f32[640,128]{1,0:T(8,128)S(1)}, u32[]{:S(2)}, u32[]{:S(2)}) collective-permute-start(f32[640,128]{1,0:T(8,128)} %get-tuple-element.22), channel_id=1, source_target_pairs={{1,0},{2,1},{3,2},{4,3},{5,4},{6,5},{7,6},{9,8},{10,9},{11,10},{12... | collective-permute-start | bytes 983048 | tf_op jit(solution)/shard_map/ppermute | solution.py:232
  72.2 4.2 %collective-permute-start.24 = (f32[20,8,128]{2,1,0:T(8,128)}, f32[20,8,128]{2,1,0:T(8,128)S(1)}, u32[]{:S(2)}, u32[]{:S(2)}) collective-permute-start(f32[20,8,128]{2,1,0:T(8,128)} %get-tuple-element.23), channel_id=1, source_target_pairs={{8,0},{16,8},{24,16},{32,24},{40,32},{48,40},{56,48},{64,56},{72,6... | collective-permute-start | bytes 245768 | tf_op jit(solution)/shard_map/ppermute | solution.py:230
  76.3 1.8 %collective-permute-done.24.right_ref = f32[20,8,128]{2,1,0:T(8,128)S(1)} collective-permute-done((f32[20,8,128]{2,1,0:T(8,128)}, f32[20,8,128]{2,1,0:T(8,128)S(1)}, u32[]{:S(2)}, u32[]{:S(2)}) %collective-permute-start.24) | collective-permute-done | bytes 81952 | tf_op jit(solution)/shard_map/ppermute | solution.py:230
  78.1 6.0 %collective-permute-done.23.left_ref = f32[20,8,128]{2,1,0:T(8,128)S(1)} collective-permute-done((f32[20,8,128]{2,1,0:T(8,128)}, f32[20,8,128]{2,1,0:T(8,128)S(1)}, u32[]{:S(2)}, u32[]{:S(2)}) %collective-permute-start.23) | collective-permute-done | bytes 81952 | tf_op jit(solution)/shard_map/ppermute | solution.py:229
  84.2 0.6 copy-done.22
  85.0 0.7 copy-done.6
  85.7 9.2 %section_one.1 = (f32[5120,128]{1,0:T(8,128)}, f32[20,8,128]{2,1,0:T(8,128)}, f32[640,128]{1,0:T(8,128)}, f32[640,128]{1,0:T(8,128)}) custom-call(f32[5120,128]{1,0:T(8,128)} %bitcast.10, f32[640,128]{1,0:T(8,128)} %copy-done.5, f32[640,128]{1,0:T(8,128)} %copy-done.6, f32[20,8,128]{2,1,0:T(8,128)} %copy-done.22, f32[20,8,128]{2,1,0:T(8,128)} %copy-done.21, ...), custom_call_target="tpu_custom_call" | custom-call | tf_op jit(solution)/shard_map/section_one/pallas_call | solution.py:269
  94.8 6.7 %collective-permute-start.25 = (f32[640,128]{1,0:T(8,128)}, f32[640,128]{1,0:T(8,128)S(1)}, u32[]{:S(2)}, u32[]{:S(2)}) collective-permute-start(f32[640,128]{1,0:T(8,128)} %get-tuple-element.25), channel_id=1, source_target_pairs={{0,1},{1,2},{2,3},{3,4},{4,5},{5,6},{6,7},{8,9},{9,10},{10,11},{11... | collective-permute-start | bytes 983048 | tf_op jit(solution)/shard_map/ppermute | solution.py:231
  101.6 1.9 %collective-permute-start.26 = (f32[640,128]{1,0:T(8,128)}, f32[640,128]{1,0:T(8,128)S(1)}, u32[]{:S(2)}, u32[]{:S(2)}) collective-permute-start(f32[640,128]{1,0:T(8,128)} %get-tuple-element.26), channel_id=1, source_target_pairs={{1,0},{2,1},{3,2},{4,3},{5,4},{6,5},{7,6},{9,8},{10,9},{11,10},{12... | collective-permute-start | bytes 983048 | tf_op jit(solution)/shard_map/ppermute | solution.py:232
  103.5 2.6 %collective-permute-start.28 = (f32[20,8,128]{2,1,0:T(8,128)}, f32[20,8,128]{2,1,0:T(8,128)S(1)}, u32[]{:S(2)}, u32[]{:S(2)}) collective-permute-start(f32[20,8,128]{2,1,0:T(8,128)} %get-tuple-element.27), channel_id=1, source_target_pairs={{8,0},{16,8},{24,16},{32,24},{40,32},{48,40},{56,48},{64,56},{72,6... | collective-permute-start | bytes 245768 | tf_op jit(solution)/shard_map/ppermute | solution.py:230
  106.1 1.5 %copy-done = bf16[64,160,128]{2,1,0:T(8,128)(2,1)} copy-done((bf16[64,160,128]{2,1,0:T(8,128)(2,1)}, bf16[64,160,128]{2,1,0:T(8,128)(2,1)S(1)}, u32[]{:S(2)}) %copy-start) | copy-done | bytes 2621464
  107.5 4.2 %face.1 = (f32[1280,128]{1,0:T(8,128)}, f32[5,8,128]{2,1,0:T(8,128)}, f32[160,128]{1,0:T(8,128)}, f32[160,128]{1,0:T(8,128)}) custom-call(s32[32]{0:T(128)} %get-tuple-element.15.slot_ref, s32[32]{0:T(128)} %bitcast.15, bf16[64,160,128]{2,1,0:T(8,128)(2,1)} %copy-done, bf16[32,128,128]{2,1,0:T(8,128)(2,1)} %bitcast.12), custom_call_target="tpu_custom_call" | custom-call | tf_op jit(solution)/shard_map/face/pallas_call | solution.py:297
  111.8 3.9 %collective-permute-start.17 = (f32[160,128]{1,0:T(8,128)}, f32[160,128]{1,0:T(8,128)S(1)}, u32[]{:S(2)}, u32[]{:S(2)}) collective-permute-start(f32[160,128]{1,0:T(8,128)} %get-tuple-element.18), channel_id=1, source_target_pairs={{0,1},{1,2},{2,3},{3,4},{4,5},{5,6},{6,7},{8,9},{9,10},{10,11},{11... | collective-permute-start | bytes 245768 | tf_op jit(solution)/shard_map/ppermute | solution.py:231
  115.7 1.9 %collective-permute-start.18 = (f32[160,128]{1,0:T(8,128)}, f32[160,128]{1,0:T(8,128)S(1)}, u32[]{:S(2)}, u32[]{:S(2)}) collective-permute-start(f32[160,128]{1,0:T(8,128)} %get-tuple-element.19), channel_id=1, source_target_pairs={{1,0},{2,1},{3,2},{4,3},{5,4},{6,5},{7,6},{9,8},{10,9},{11,10},{12... | collective-permute-start | bytes 245768 | tf_op jit(solution)/shard_map/ppermute | solution.py:232
  117.7 5.1 %collective-permute-start.20 = (f32[5,8,128]{2,1,0:T(8,128)}, f32[5,8,128]{2,1,0:T(8,128)S(1)}, u32[]{:S(2)}, u32[]{:S(2)}) collective-permute-start(f32[5,8,128]{2,1,0:T(8,128)} %get-tuple-element.20), channel_id=1, source_target_pairs={{8,0},{16,8},{24,16},{32,24},{40,32},{48,40},{56,48},{64,56},{72,6... | collective-permute-start | bytes 61448 | tf_op jit(solution)/shard_map/ppermute | solution.py:230
  122.8 0.7 copy-done.3
  123.6 7.7 %section_two.1.part_ref = f32[5120,128]{1,0:T(8,128)} custom-call(f32[5120,128]{1,0:T(8,128)} %get-tuple-element.24.v_ref, f32[640,128]{1,0:T(8,128)} %copy-done.3, f32[640,128]{1,0:T(8,128)} %copy-done.4, f32[20,8,128]{2,1,0:T(8,128)} %copy-done.25, f32[20,8,128]{2,1,0:T(8,128)} %copy-done.23, f32[8,128]{1,0:T(8,128)} %damp_ref.5), custom_call_target="tpu_custom_call" | custom-call | tf_op jit(solution)/shard_map/section_two/pallas_call | solution.py:277
  131.3 0.5 copy-done.27
  132.0 3.8 %finish.1 = f32[5120,128]{1,0:T(8,128)} custom-call(f32[1280,128]{1,0:T(8,128)} %get-tuple-element.17.face_ref, f32[160,128]{1,0:T(8,128)} %copy-done.24, f32[160,128]{1,0:T(8,128)} %copy-done.26, f32[5,8,128]{2,1,0:T(8,128)} %copy-done.28, f32[5,8,128]{2,1,0:T(8,128)} %copy-done.27, f32[8,128]{1,0:T(8,128)} %damp_ref.5, ...), custom_call_target="tpu_custom_call", output_to_operand_aliasing={{}: (6, {})} | custom-call | tf_op jit(solution)/shard_map/finish/pallas_call | solution.py:307
  (88 shorter events, 0.7 us)
Async XLA Ops:
  1.7 44.1 %copy-start.1 = (bf16[8,80,128]{2,1,0:T(8,128)(2,1)}, bf16[8,80,128]{2,1,0:T(8,128)(2,1)S(1)}, u32[]{:S(2)}) copy-start(bf16[8,80,128]{2,1,0:T(8,128)(2,1)S(1)} %get-tuple-element.28.refs_1_) | copy-start | bytes 491524
  1.7 44.1 %copy-start.2 = (bf16[8,80,128]{2,1,0:T(8,128)(2,1)}, bf16[8,80,128]{2,1,0:T(8,128)(2,1)S(1)}, u32[]{:S(2)}) copy-start(bf16[8,80,128]{2,1,0:T(8,128)(2,1)S(1)} %get-tuple-element.29.refs_0_) | copy-start | bytes 491524
  1.7 9.4 %collective-permute-start.6 = (bf16[8,80,128]{2,1,0:T(8,128)(2,1)S(1)}, bf16[8,80,128]{2,1,0:T(8,128)(2,1)S(1)}, u32[]{:S(2)}, u32[]{:S(2)}) collective-permute-start(bf16[8,80,128]{2,1,0:T(8,128)(2,1)S(1)} %get-tuple-element.28.refs_1_), channel_id=1, source_target_pairs={{0,224},{8,232},{16,240},{24,248},{32,0},{40,8},{48,16},{56,24},{6... | collective-permute-start | bytes 491528 | tf_op jit(solution)/shard_map/ppermute | solution.py:242
  8.1 6.3 %collective-permute-start.3 = (bf16[8,80,128]{2,1,0:T(8,128)(2,1)S(1)}, bf16[8,80,128]{2,1,0:T(8,128)(2,1)S(1)}, u32[]{:S(2)}, u32[]{:S(2)}) collective-permute-start(bf16[8,80,128]{2,1,0:T(8,128)(2,1)S(1)} %get-tuple-element.29.refs_0_), channel_id=1, source_target_pairs={{0,32},{8,40},{16,48},{24,56},{32,64},{40,72},{48,80},{56,88},{64,... | collective-permute-start | bytes 491528 | tf_op jit(solution)/shard_map/ppermute | solution.py:241
  8.2 9.5 %collective-permute-start.4 = (bf16[8,80,128]{2,1,0:T(8,128)(2,1)S(1)}, bf16[8,80,128]{2,1,0:T(8,128)(2,1)S(1)}, u32[]{:S(2)}, u32[]{:S(2)}) collective-permute-start(bf16[8,80,128]{2,1,0:T(8,128)(2,1)S(1)} %get-tuple-element.28.refs_1_), channel_id=1, source_target_pairs={{0,32},{8,40},{16,48},{24,56},{32,64},{40,72},{48,80},{56,88},{64,... | collective-permute-start | bytes 491528 | tf_op jit(solution)/shard_map/ppermute | solution.py:241
  8.2 9.5 %collective-permute-start.5 = (bf16[8,80,128]{2,1,0:T(8,128)(2,1)S(1)}, bf16[8,80,128]{2,1,0:T(8,128)(2,1)S(1)}, u32[]{:S(2)}, u32[]{:S(2)}) collective-permute-start(bf16[8,80,128]{2,1,0:T(8,128)(2,1)S(1)} %get-tuple-element.29.refs_0_), channel_id=1, source_target_pairs={{0,224},{8,232},{16,240},{24,248},{32,0},{40,8},{48,16},{56,24},{6... | collective-permute-start | bytes 491528 | tf_op jit(solution)/shard_map/ppermute | solution.py:242
  11.0 34.7 %copy-start.7 = (bf16[8,80,128]{2,1,0:T(8,128)(2,1)}, bf16[8,80,128]{2,1,0:T(8,128)(2,1)S(1)}, u32[]{:S(2)}) copy-start(bf16[8,80,128]{2,1,0:T(8,128)(2,1)S(1)} %collective-permute-done.6.refs_5_) | copy-start | bytes 491524
  11.0 9.3 %collective-permute-start.10 = (bf16[8,80,128]{2,1,0:T(8,128)(2,1)S(1)}, bf16[8,80,128]{2,1,0:T(8,128)(2,1)S(1)}, u32[]{:S(2)}, u32[]{:S(2)}) collective-permute-start(bf16[8,80,128]{2,1,0:T(8,128)(2,1)S(1)} %collective-permute-done.6.refs_5_), channel_id=1, source_target_pairs={{0,224},{8,232},{16,240},{24,248},{32,0},{40,8},{48,16},{56,24},{6... | collective-permute-start | bytes 491528 | tf_op jit(solution)/shard_map/ppermute | solution.py:242
  14.4 31.3 %copy-start.8 = (bf16[8,80,128]{2,1,0:T(8,128)(2,1)}, bf16[8,80,128]{2,1,0:T(8,128)(2,1)S(1)}, u32[]{:S(2)}) copy-start(bf16[8,80,128]{2,1,0:T(8,128)(2,1)S(1)} %collective-permute-done.3.refs_2_) | copy-start | bytes 491524
  14.5 6.1 %collective-permute-start.7 = (bf16[8,80,128]{2,1,0:T(8,128)(2,1)S(1)}, bf16[8,80,128]{2,1,0:T(8,128)(2,1)S(1)}, u32[]{:S(2)}, u32[]{:S(2)}) collective-permute-start(bf16[8,80,128]{2,1,0:T(8,128)(2,1)S(1)} %collective-permute-done.3.refs_2_), channel_id=1, source_target_pairs={{0,32},{8,40},{16,48},{24,56},{32,64},{40,72},{48,80},{56,88},{64,... | collective-permute-start | bytes 491528 | tf_op jit(solution)/shard_map/ppermute | solution.py:241
  17.7 28.1 %copy-start.9 = (bf16[8,80,128]{2,1,0:T(8,128)(2,1)}, bf16[8,80,128]{2,1,0:T(8,128)(2,1)S(1)}, u32[]{:S(2)}) copy-start(bf16[8,80,128]{2,1,0:T(8,128)(2,1)S(1)} %collective-permute-done.4.refs_3_) | copy-start | bytes 491524
  17.7 7.3 %collective-permute-start.8 = (bf16[8,80,128]{2,1,0:T(8,128)(2,1)S(1)}, bf16[8,80,128]{2,1,0:T(8,128)(2,1)S(1)}, u32[]{:S(2)}, u32[]{:S(2)}) collective-permute-start(bf16[8,80,128]{2,1,0:T(8,128)(2,1)S(1)} %collective-permute-done.4.refs_3_), channel_id=1, source_target_pairs={{0,32},{8,40},{16,48},{24,56},{32,64},{40,72},{48,80},{56,88},{64,... | collective-permute-start | bytes 491528 | tf_op jit(solution)/shard_map/ppermute | solution.py:241
  17.7 28.1 %copy-start.10 = (bf16[8,80,128]{2,1,0:T(8,128)(2,1)}, bf16[8,80,128]{2,1,0:T(8,128)(2,1)S(1)}, u32[]{:S(2)}) copy-start(bf16[8,80,128]{2,1,0:T(8,128)(2,1)S(1)} %collective-permute-done.5.refs_4_) | copy-start | bytes 491524
  17.7 7.2 %collective-permute-start.9 = (bf16[8,80,128]{2,1,0:T(8,128)(2,1)S(1)}, bf16[8,80,128]{2,1,0:T(8,128)(2,1)S(1)}, u32[]{:S(2)}, u32[]{:S(2)}) collective-permute-start(bf16[8,80,128]{2,1,0:T(8,128)(2,1)S(1)} %collective-permute-done.5.refs_4_), channel_id=1, source_target_pairs={{0,224},{8,232},{16,240},{24,248},{32,0},{40,8},{48,16},{56,24},{6... | collective-permute-start | bytes 491528 | tf_op jit(solution)/shard_map/ppermute | solution.py:242
  20.4 25.4 %copy-start.11 = (bf16[8,80,128]{2,1,0:T(8,128)(2,1)}, bf16[8,80,128]{2,1,0:T(8,128)(2,1)S(1)}, u32[]{:S(2)}) copy-start(bf16[8,80,128]{2,1,0:T(8,128)(2,1)S(1)} %collective-permute-done.10.refs_9_) | copy-start | bytes 491524
  20.4 7.3 %collective-permute-start.14 = (bf16[8,80,128]{2,1,0:T(8,128)(2,1)S(1)}, bf16[8,80,128]{2,1,0:T(8,128)(2,1)S(1)}, u32[]{:S(2)}, u32[]{:S(2)}) collective-permute-start(bf16[8,80,128]{2,1,0:T(8,128)(2,1)S(1)} %collective-permute-done.10.refs_9_), channel_id=1, source_target_pairs={{0,224},{8,232},{16,240},{24,248},{32,0},{40,8},{48,16},{56,24},{6... | collective-permute-start | bytes 491528 | tf_op jit(solution)/shard_map/ppermute | solution.py:242
  20.6 25.2 %copy-start.12 = (bf16[8,80,128]{2,1,0:T(8,128)(2,1)}, bf16[8,80,128]{2,1,0:T(8,128)(2,1)S(1)}, u32[]{:S(2)}) copy-start(bf16[8,80,128]{2,1,0:T(8,128)(2,1)S(1)} %collective-permute-done.7.refs_6_) | copy-start | bytes 491524
  20.6 7.9 %collective-permute-start.11 = (bf16[8,80,128]{2,1,0:T(8,128)(2,1)S(1)}, bf16[8,80,128]{2,1,0:T(8,128)(2,1)S(1)}, u32[]{:S(2)}, u32[]{:S(2)}) collective-permute-start(bf16[8,80,128]{2,1,0:T(8,128)(2,1)S(1)} %collective-permute-done.7.refs_6_), channel_id=1, source_target_pairs={{0,32},{8,40},{16,48},{24,56},{32,64},{40,72},{48,80},{56,88},{64,... | collective-permute-start | bytes 491528 | tf_op jit(solution)/shard_map/ppermute | solution.py:241
  24.9 20.9 %copy-start.13 = (bf16[8,80,128]{2,1,0:T(8,128)(2,1)}, bf16[8,80,128]{2,1,0:T(8,128)(2,1)S(1)}, u32[]{:S(2)}) copy-start(bf16[8,80,128]{2,1,0:T(8,128)(2,1)S(1)} %collective-permute-done.8.refs_7_) | copy-start | bytes 491524
  24.9 20.7 %collective-permute-start.12 = (bf16[8,80,128]{2,1,0:T(8,128)(2,1)S(1)}, bf16[8,80,128]{2,1,0:T(8,128)(2,1)S(1)}, u32[]{:S(2)}, u32[]{:S(2)}) collective-permute-start(bf16[8,80,128]{2,1,0:T(8,128)(2,1)S(1)} %collective-permute-done.8.refs_7_), channel_id=1, source_target_pairs={{0,32},{8,40},{16,48},{24,56},{32,64},{40,72},{48,80},{56,88},{64,... | collective-permute-start | bytes 491528 | tf_op jit(solution)/shard_map/ppermute | solution.py:241
  24.9 20.9 %copy-start.14 = (bf16[8,80,128]{2,1,0:T(8,128)(2,1)}, bf16[8,80,128]{2,1,0:T(8,128)(2,1)S(1)}, u32[]{:S(2)}) copy-start(bf16[8,80,128]{2,1,0:T(8,128)(2,1)S(1)} %collective-permute-done.9.refs_8_) | copy-start | bytes 491524
  25.0 20.7 %collective-permute-start.13 = (bf16[8,80,128]{2,1,0:T(8,128)(2,1)S(1)}, bf16[8,80,128]{2,1,0:T(8,128)(2,1)S(1)}, u32[]{:S(2)}, u32[]{:S(2)}) collective-permute-start(bf16[8,80,128]{2,1,0:T(8,128)(2,1)S(1)} %collective-permute-done.9.refs_8_), channel_id=1, source_target_pairs={{0,224},{8,232},{16,240},{24,248},{32,0},{40,8},{48,16},{56,24},{6... | collective-permute-start | bytes 491528 | tf_op jit(solution)/shard_map/ppermute | solution.py:242
  27.6 18.2 %copy-start.15 = (bf16[8,80,128]{2,1,0:T(8,128)(2,1)}, bf16[8,80,128]{2,1,0:T(8,128)(2,1)S(1)}, u32[]{:S(2)}) copy-start(bf16[8,80,128]{2,1,0:T(8,128)(2,1)S(1)} %collective-permute-done.14.refs_13_) | copy-start | bytes 491524
  27.6 18.0 %collective-permute-start.16 = (bf16[8,80,128]{2,1,0:T(8,128)(2,1)S(1)}, bf16[8,80,128]{2,1,0:T(8,128)(2,1)S(1)}, u32[]{:S(2)}, u32[]{:S(2)}) collective-permute-start(bf16[8,80,128]{2,1,0:T(8,128)(2,1)S(1)} %collective-permute-done.14.refs_13_), channel_id=1, source_target_pairs={{0,224},{8,232},{16,240},{24,248},{32,0},{40,8},{48,16},{56,24},{6... | collective-permute-start | bytes 491528 | tf_op jit(solution)/shard_map/ppermute | solution.py:246
  28.4 17.4 %copy-start.16 = (bf16[8,80,128]{2,1,0:T(8,128)(2,1)}, bf16[8,80,128]{2,1,0:T(8,128)(2,1)S(1)}, u32[]{:S(2)}) copy-start(bf16[8,80,128]{2,1,0:T(8,128)(2,1)S(1)} %collective-permute-done.11.refs_10_) | copy-start | bytes 491524
  28.5 17.2 %collective-permute-start.15 = (bf16[8,80,128]{2,1,0:T(8,128)(2,1)S(1)}, bf16[8,80,128]{2,1,0:T(8,128)(2,1)S(1)}, u32[]{:S(2)}, u32[]{:S(2)}) collective-permute-start(bf16[8,80,128]{2,1,0:T(8,128)(2,1)S(1)} %collective-permute-done.11.refs_10_), channel_id=1, source_target_pairs={{0,32},{8,40},{16,48},{24,56},{32,64},{40,72},{48,80},{56,88},{64,... | collective-permute-start | bytes 491528 | tf_op jit(solution)/shard_map/ppermute | solution.py:245
  29.8 10.4 %copy-start.29 = (s32[2,32]{1,0:T(2,128)}, s32[2,32]{1,0:T(2,128)S(1)}, u32[]{:S(2)}) copy-start(s32[2,32]{1,0:T(2,128)S(1)} %pad_add_fusion.own_ref) | copy-start | bytes 772
  29.8 4.1 %collective-permute-start.2 = (s32[2,32]{1,0:T(2,128)S(1)}, s32[2,32]{1,0:T(2,128)S(1)}, u32[]{:S(2)}, u32[]{:S(2)}) collective-permute-start(s32[2,32]{1,0:T(2,128)S(1)} %pad_add_fusion.own_ref), channel_id=1, source_target_pairs={{0,8},{8,16},{16,24},{24,0},{32,40},{40,48},{48,56},{56,32},{64,72... | collective-permute-start | bytes 776 | tf_op jit(solution)/shard_map/ppermute | solution.py:236
  33.9 6.4 %copy-start.30 = (s32[2,32]{1,0:T(2,128)}, s32[2,32]{1,0:T(2,128)S(1)}, u32[]{:S(2)}) copy-start(s32[2,32]{1,0:T(2,128)S(1)} %collective-permute-done.2.back_ref) | copy-start | bytes 772
  33.9 3.9 %collective-permute-start.1 = (s32[2,32]{1,0:T(2,128)S(1)}, s32[2,32]{1,0:T(2,128)S(1)}, u32[]{:S(2)}, u32[]{:S(2)}) collective-permute-start(s32[2,32]{1,0:T(2,128)S(1)} %pad_add_fusion.own_ref), channel_id=1, source_target_pairs={{0,16},{8,24},{16,0},{24,8},{32,48},{40,56},{48,32},{56,40},{64,80... | collective-permute-start | bytes 776 | tf_op jit(solution)/shard_map/ppermute | solution.py:236
  37.8 2.4 %copy-start.31 = (s32[2,32]{1,0:T(2,128)}, s32[2,32]{1,0:T(2,128)S(1)}, u32[]{:S(2)}) copy-start(s32[2,32]{1,0:T(2,128)S(1)} %collective-permute-done.1.far_ref) | copy-start | bytes 772
  37.8 2.4 %collective-permute-start = (s32[2,32]{1,0:T(2,128)S(1)}, s32[2,32]{1,0:T(2,128)S(1)}, u32[]{:S(2)}, u32[]{:S(2)}) collective-permute-start(s32[2,32]{1,0:T(2,128)S(1)} %pad_add_fusion.own_ref), channel_id=1, source_target_pairs={{0,24},{8,0},{16,8},{24,16},{32,56},{40,32},{48,40},{56,48},{64,88... | collective-permute-start | bytes 776 | tf_op jit(solution)/shard_map/ppermute | solution.py:236
  50.0 56.1 %all-to-all-start = ((bf16[64,160,128]{2,1,0:T(8,128)(2,1)}), bf16[64,160,128]{2,1,0:T(8,128)(2,1)S(1)}, u32[]{:S(2)}, u32[]{:S(2)}) async-start(bf16[64,160,128]{2,1,0:T(8,128)(2,1)} %select.7), calls=%async_computation | async-start | bytes 5242880 | tf_op jit(solution)/shard_map/all_to_all | solution.py:296
  58.6 25.6 %collective-permute-start.21 = (f32[640,128]{1,0:T(8,128)}, f32[640,128]{1,0:T(8,128)S(1)}, u32[]{:S(2)}, u32[]{:S(2)}) collective-permute-start(f32[640,128]{1,0:T(8,128)} %get-tuple-element.21), channel_id=1, source_target_pairs={{0,1},{1,2},{2,3},{3,4},{4,5},{5,6},{6,7},{8,9},{9,10},{10,11},{11... | collective-permute-start | bytes 983048 | tf_op jit(solution)/shard_map/ppermute | solution.py:231
  70.2 14.0 %collective-permute-start.22 = (f32[640,128]{1,0:T(8,128)}, f32[640,128]{1,0:T(8,128)S(1)}, u32[]{:S(2)}, u32[]{:S(2)}) collective-permute-start(f32[640,128]{1,0:T(8,128)} %get-tuple-element.22), channel_id=1, source_target_pairs={{1,0},{2,1},{3,2},{4,3},{5,4},{6,5},{7,6},{9,8},{10,9},{11,10},{12... | collective-permute-start | bytes 983048 | tf_op jit(solution)/shard_map/ppermute | solution.py:232
  72.2 6.0 %collective-permute-start.24 = (f32[20,8,128]{2,1,0:T(8,128)}, f32[20,8,128]{2,1,0:T(8,128)S(1)}, u32[]{:S(2)}, u32[]{:S(2)}) collective-permute-start(f32[20,8,128]{2,1,0:T(8,128)} %get-tuple-element.23), channel_id=1, source_target_pairs={{8,0},{16,8},{24,16},{32,24},{40,32},{48,40},{56,48},{64,56},{72,6... | collective-permute-start | bytes 245768 | tf_op jit(solution)/shard_map/ppermute | solution.py:230
  76.3 7.9 %collective-permute-start.23 = (f32[20,8,128]{2,1,0:T(8,128)}, f32[20,8,128]{2,1,0:T(8,128)S(1)}, u32[]{:S(2)}, u32[]{:S(2)}) collective-permute-start(f32[20,8,128]{2,1,0:T(8,128)} %get-tuple-element.23), channel_id=1, source_target_pairs={{0,8},{8,16},{16,24},{24,32},{32,40},{40,48},{48,56},{56,64},{64,7... | collective-permute-start | bytes 245768 | tf_op jit(solution)/shard_map/ppermute | solution.py:229
  78.1 6.1 %copy-start.21 = (f32[20,8,128]{2,1,0:T(8,128)}, f32[20,8,128]{2,1,0:T(8,128)S(1)}, u32[]{:S(2)}) copy-start(f32[20,8,128]{2,1,0:T(8,128)S(1)} %collective-permute-done.24.right_ref) | copy-start | bytes 245764
  94.8 28.0 %collective-permute-start.25 = (f32[640,128]{1,0:T(8,128)}, f32[640,128]{1,0:T(8,128)S(1)}, u32[]{:S(2)}, u32[]{:S(2)}) collective-permute-start(f32[640,128]{1,0:T(8,128)} %get-tuple-element.25), channel_id=1, source_target_pairs={{0,1},{1,2},{2,3},{3,4},{4,5},{5,6},{6,7},{8,9},{9,10},{10,11},{11... | collective-permute-start | bytes 983048 | tf_op jit(solution)/shard_map/ppermute | solution.py:231
  101.6 21.2 %collective-permute-start.26 = (f32[640,128]{1,0:T(8,128)}, f32[640,128]{1,0:T(8,128)S(1)}, u32[]{:S(2)}, u32[]{:S(2)}) collective-permute-start(f32[640,128]{1,0:T(8,128)} %get-tuple-element.26), channel_id=1, source_target_pairs={{1,0},{2,1},{3,2},{4,3},{5,4},{6,5},{7,6},{9,8},{10,9},{11,10},{12... | collective-permute-start | bytes 983048 | tf_op jit(solution)/shard_map/ppermute | solution.py:232
  103.5 12.2 %collective-permute-start.28 = (f32[20,8,128]{2,1,0:T(8,128)}, f32[20,8,128]{2,1,0:T(8,128)S(1)}, u32[]{:S(2)}, u32[]{:S(2)}) collective-permute-start(f32[20,8,128]{2,1,0:T(8,128)} %get-tuple-element.27), channel_id=1, source_target_pairs={{8,0},{16,8},{24,16},{32,24},{40,32},{48,40},{56,48},{64,56},{72,6... | collective-permute-start | bytes 245768 | tf_op jit(solution)/shard_map/ppermute | solution.py:230
  106.0 11.6 %collective-permute-start.27 = (f32[20,8,128]{2,1,0:T(8,128)}, f32[20,8,128]{2,1,0:T(8,128)S(1)}, u32[]{:S(2)}, u32[]{:S(2)}) collective-permute-start(f32[20,8,128]{2,1,0:T(8,128)} %get-tuple-element.27), channel_id=1, source_target_pairs={{0,8},{8,16},{16,24},{24,32},{32,40},{40,48},{48,56},{56,64},{64,7... | collective-permute-start | bytes 245768 | tf_op jit(solution)/shard_map/ppermute | solution.py:229
  111.8 19.5 %collective-permute-start.17 = (f32[160,128]{1,0:T(8,128)}, f32[160,128]{1,0:T(8,128)S(1)}, u32[]{:S(2)}, u32[]{:S(2)}) collective-permute-start(f32[160,128]{1,0:T(8,128)} %get-tuple-element.18), channel_id=1, source_target_pairs={{0,1},{1,2},{2,3},{3,4},{4,5},{5,6},{6,7},{8,9},{9,10},{10,11},{11... | collective-permute-start | bytes 245768 | tf_op jit(solution)/shard_map/ppermute | solution.py:231
  115.7 7.1 %copy-start.23 = (f32[20,8,128]{2,1,0:T(8,128)}, f32[20,8,128]{2,1,0:T(8,128)S(1)}, u32[]{:S(2)}) copy-start(f32[20,8,128]{2,1,0:T(8,128)S(1)} %collective-permute-done.28.right_ref) | copy-start | bytes 245764
  115.7 15.6 %collective-permute-start.18 = (f32[160,128]{1,0:T(8,128)}, f32[160,128]{1,0:T(8,128)S(1)}, u32[]{:S(2)}, u32[]{:S(2)}) collective-permute-start(f32[160,128]{1,0:T(8,128)} %get-tuple-element.19), channel_id=1, source_target_pairs={{1,0},{2,1},{3,2},{4,3},{5,4},{6,5},{7,6},{9,8},{10,9},{11,10},{12... | collective-permute-start | bytes 245768 | tf_op jit(solution)/shard_map/ppermute | solution.py:232
  117.6 5.2 %copy-start.25 = (f32[20,8,128]{2,1,0:T(8,128)}, f32[20,8,128]{2,1,0:T(8,128)S(1)}, u32[]{:S(2)}) copy-start(f32[20,8,128]{2,1,0:T(8,128)S(1)} %collective-permute-done.27.left_ref) | copy-start | bytes 245764
  117.7 13.6 %collective-permute-start.20 = (f32[5,8,128]{2,1,0:T(8,128)}, f32[5,8,128]{2,1,0:T(8,128)S(1)}, u32[]{:S(2)}, u32[]{:S(2)}) collective-permute-start(f32[5,8,128]{2,1,0:T(8,128)} %get-tuple-element.20), channel_id=1, source_target_pairs={{8,0},{16,8},{24,16},{32,24},{40,32},{48,40},{56,48},{64,56},{72,6... | collective-permute-start | bytes 61448 | tf_op jit(solution)/shard_map/ppermute | solution.py:230
  122.8 8.5 %collective-permute-start.19 = (f32[5,8,128]{2,1,0:T(8,128)}, f32[5,8,128]{2,1,0:T(8,128)S(1)}, u32[]{:S(2)}, u32[]{:S(2)}) collective-permute-start(f32[5,8,128]{2,1,0:T(8,128)} %get-tuple-element.20), channel_id=1, source_target_pairs={{0,8},{8,16},{16,24},{24,32},{32,40},{40,48},{48,56},{56,64},{64,7... | collective-permute-start | bytes 61448 | tf_op jit(solution)/shard_map/ppermute | solution.py:229
  (15 other events, 11.1 us)
